TPU v7x, 32 devices: a whole 2x2x4 slice. The times are simulated.
32 devices in a mesh: grp: 2 (over x), mem: 16 (over z, y, core).
Axes of the slice: x: 2, y: 2, z: 4, core: 2. Of those that a mesh axis runs over, the one named last changes fastest.
Arguments:
- field: bfloat16 [128, 16, 64, 256], P(('grp', 'mem')), parts along dimension 0, may hold values from -8 to 8
- norm_gain: float32 [2, 2, 256], replicated, may hold values from 0.1 to 1.9
- conv_weight: bfloat16 [2, 3, 3, 256, 512], replicated, may hold values from -0.125 to 0.125
- qkv_weight: bfloat16 [2, 256, 768], replicated, may hold values from -8 to 8
- out_weight: bfloat16 [2, 256, 256], replicated, may hold values from -0.375 to 0.375
Outputs:
- result: bfloat16 [128, 16, 64, 256], P(('grp', 'mem')), parts along dimension 0
There are 2 independent parts, one for each index of `grp`. A program takes and returns all parts, laid end to end along the dimension named above; an argument that names none is the same for every part. Nothing has to cross between parts.
All inputs are finite; a program needn't handle non-finite values.
Results may differ from a plain program's by a relative error of at most 0.014.
Values may be sent and summed in bfloat16 or wider, within the bound.
A program may use at most 128 MiB of HBM per device.

v0:
```python
import functools

import jax
import jax.numpy as jnp
from jax import lax
from jax.experimental import pallas as pl
from jax.experimental.pallas import tpu as pltpu
from jax.sharding import PartitionSpec as P

HEADS = 8
BLOCKS = 2
epsilon = 1e-06
VMEM_LIMIT = 58 * 1024 * 1024


def normalised(x, gain):
    inverse = lax.rsqrt(jnp.mean(x * x, axis=-1, keepdims=True) + epsilon)
    return x * inverse * gain


def gated(x, conv_out):
    channels = x.shape[-1]
    gate = conv_out[:, channels:]
    return x + conv_out[:, :channels] * (1.0 / (1.0 + jnp.exp(-gate)))


def taps(wide_ref, weight_ref, row, step):
    total = None
    for di in range(3):
        lhs = wide_ref[pl.ds(row + di, step)]
        lhs = lhs.reshape(-1, lhs.shape[-1])
        part = jnp.dot(lhs, weight_ref[di], preferred_element_type=jnp.float32)
        total = part if total is None else total + part
    return total


def conv_member_kernel(x_ref, gain_ref, weight_ref, out_ref, wide_ref):
    _, rows, cols, channels = x_ref.shape
    step = min(rows, 4)
    big = min(rows, 8)
    gain = gain_ref[...]
    zero = jnp.zeros((1, cols, 3 * channels), jnp.bfloat16)
    wide_ref[0:1] = zero
    wide_ref[rows + 1 : rows + 2] = zero
    flat = step * cols
    column = lax.broadcasted_iota(jnp.int32, (flat, channels), 0) % cols
    for row in range(0, rows, step):
        x = x_ref[0, row : row + step].astype(jnp.float32).reshape(flat, channels)
        normed = normalised(x, gain)
        left = jnp.where(column == 0, 0.0, pltpu.roll(normed, 1, 0))
        right = jnp.where(column == cols - 1, 0.0, pltpu.roll(normed, flat - 1, 0))
        for at, value in enumerate((left, normed, right)):
            wide_ref[row + 1 : row + 1 + step, :, at * channels : (at + 1) * channels] = value.astype(
                jnp.bfloat16
            ).reshape(step, cols, channels)
    for row in range(0, rows, big):
        conv_out = taps(wide_ref, weight_ref, row, big)
        x = x_ref[0, row : row + big].astype(jnp.float32).reshape(big * cols, channels)
        out_ref[0, row : row + big] = (
            gated(x, conv_out).astype(jnp.bfloat16).reshape(big, cols, channels)
        )


def conv_member(field, gain_row, weight):
    members, rows, cols, channels = field.shape
    weight = weight.reshape(3, 3 * channels, 2 * channels)
    return pl.pallas_call(
        conv_member_kernel,
        grid=(members,),
        in_specs=[
            pl.BlockSpec((1, rows, cols, channels), lambda i: (i, 0, 0, 0)),
            pl.BlockSpec((1, channels), lambda i: (0, 0)),
            pl.BlockSpec((3, 3 * channels, 2 * channels), lambda i: (0, 0, 0)),
        ],
        out_specs=pl.BlockSpec((1, rows, cols, channels), lambda i: (i, 0, 0, 0)),
        out_shape=jax.ShapeDtypeStruct(field.shape, jnp.bfloat16),
        scratch_shapes=[pltpu.VMEM((rows + 2, cols, 3 * channels), jnp.bfloat16)],
        compiler_params=pltpu.CompilerParams(vmem_limit_bytes=VMEM_LIMIT),
        name="conv_member",
    )(field, gain_row.reshape(1, channels), weight)


def conv_cell_kernel(x_ref, left_ref, right_ref, gain_ref, weight_ref, out_ref, wide_ref):
    rows, cols, members, channels = x_ref.shape
    gain = gain_ref[...]
    zero = jnp.zeros((1, cols, members, 3 * channels), jnp.bfloat16)
    wide_ref[0:1] = zero
    wide_ref[rows + 1 : rows + 2] = zero

    @pl.loop(0, rows)
    def _(row):
        def normed_of(ref, col):
            x = ref[row, col].astype(jnp.float32)
            return normalised(x, gain).astype(jnp.bfloat16)

        for col in range(-1, cols + 1):
            if col < 0:
                value = normed_of(left_ref, 0)
            elif col == cols:
                value = normed_of(right_ref, 0)
            else:
                value = normed_of(x_ref, col)
            for dj in range(3):
                target = col + 1 - dj
                if 0 <= target < cols:
                    wide_ref[row + 1, target, :, dj * channels : (dj + 1) * channels] = value

    step = max(1, min(rows, 512 // (cols * members)))

    @pl.loop(0, rows // step)
    def _(index):
        row = index * step
        conv_out = taps(wide_ref, weight_ref, row, step)
        x = x_ref[pl.ds(row, step)].astype(jnp.float32).reshape(-1, channels)
        out_ref[pl.ds(row, step)] = (
            gated(x, conv_out).astype(jnp.bfloat16).reshape(step, cols, members, channels)
        )


def conv_cell(state, left, right, gain_row, weight):
    rows, cols, members, channels = state.shape
    weight = weight.reshape(3, 3 * channels, 2 * channels)
    return pl.pallas_call(
        conv_cell_kernel,
        in_specs=[pl.BlockSpec(memory_space=pltpu.VMEM)] * 5,
        out_specs=pl.BlockSpec(memory_space=pltpu.VMEM),
        out_shape=jax.ShapeDtypeStruct(state.shape, jnp.bfloat16),
        scratch_shapes=[pltpu.VMEM((rows + 2, cols, members, 3 * channels), jnp.bfloat16)],
        compiler_params=pltpu.CompilerParams(vmem_limit_bytes=VMEM_LIMIT),
        name="conv_cell",
    )(state, left, right, gain_row.reshape(1, channels), weight)


def attend_block(x, gain, qkv_ref, out_w_ref, ones_ref):
    cells, members, channels = x.shape
    head_size = channels // HEADS
    scale = head_size ** (-0.5)
    rows = x.astype(jnp.float32).reshape(cells * members, channels)
    normed = normalised(rows, gain).astype(jnp.bfloat16)
    projected = jnp.dot(normed, qkv_ref[...], preferred_element_type=jnp.float32).astype(
        jnp.bfloat16
    )
    lane_head = lax.broadcasted_iota(jnp.int32, (members, channels), 1) // head_size
    masks = [lane_head == h for h in range(HEADS)]
    zero = jnp.zeros((members, channels), jnp.bfloat16)
    per = max(1, 128 // members)
    width = per * members
    lane_slot = lax.broadcasted_iota(jnp.int32, (members, width), 1) // members
    weights, mixed = [], []
    for cell in range(cells):
        block = projected[cell * members : (cell + 1) * members]
        queries = block[:, :channels]
        keys = block[:, channels : 2 * channels]
        values = block[:, 2 * channels :]
        spread_keys = jnp.concatenate([jnp.where(m, keys, zero) for m in masks], axis=0)
        spread_values = jnp.concatenate([jnp.where(m, values, zero) for m in masks], axis=0)
        scores = lax.dot_general(
            queries, spread_keys, (((1,), (1,)), ((), ())), preferred_element_type=jnp.float32
        )
        parts = []
        for tile in range(HEADS // per):
            s = scores[:, tile * width : (tile + 1) * width]
            if per == 1:
                most = jnp.max(s, axis=-1, keepdims=True)
            else:
                most = jnp.zeros_like(s)
                for slot in range(per):
                    here = lane_slot == slot
                    top = jnp.max(jnp.where(here, s, -jnp.inf), axis=-1, keepdims=True)
                    most = jnp.where(here, top, most)
            parts.append(jnp.exp((s - most) * scale).astype(jnp.bfloat16))
        weight = jnp.concatenate(parts, axis=1)
        weights.append(weight)
        mixed.append(jnp.dot(weight, spread_values, preferred_element_type=jnp.float32))
    weight = jnp.concatenate(weights, axis=0)
    total = jnp.dot(weight, ones_ref[...], preferred_element_type=jnp.float32)
    attended = (jnp.concatenate(mixed, axis=0) / total).astype(jnp.bfloat16)
    update = jnp.dot(attended, out_w_ref[...], preferred_element_type=jnp.float32)
    return (rows + update).astype(jnp.bfloat16).reshape(x.shape)


def attend_kernel(x_ref, gain_ref, qkv_ref, out_w_ref, ones_ref, out_ref):
    out_ref[...] = attend_block(x_ref[...], gain_ref[...], qkv_ref, out_w_ref, ones_ref)


def head_sums(members, channels):
    row = jnp.arange(HEADS * members)[:, None] // members
    lane = jnp.arange(channels)[None, :] // (channels // HEADS)
    return (row == lane).astype(jnp.bfloat16)


def attend(state, gain_row, qkv, out_w):
    cells, members, channels = state.shape
    block = max(1, min(cells, 512 // members))
    spec = pl.BlockSpec((block, members, channels), lambda i: (i, 0, 0))
    return pl.pallas_call(
        attend_kernel,
        grid=(cells // block,),
        in_specs=[
            spec,
            pl.BlockSpec((1, channels), lambda i: (0, 0)),
            pl.BlockSpec((channels, 3 * channels), lambda i: (0, 0)),
            pl.BlockSpec((channels, channels), lambda i: (0, 0)),
            pl.BlockSpec((HEADS * members, channels), lambda i: (0, 0)),
        ],
        out_specs=spec,
        out_shape=jax.ShapeDtypeStruct(state.shape, jnp.bfloat16),
        compiler_params=pltpu.CompilerParams(vmem_limit_bytes=VMEM_LIMIT),
        name="attend",
    )(state, gain_row.reshape(1, channels), qkv, out_w, head_sums(members, channels))


def body(field, norm_gain, conv_weight, qkv_weight, out_weight):
    members, rows, cols, channels = field.shape
    devices = lax.axis_size("mem")
    width = cols // devices
    all_members = members * devices
    forward = [(i, i + 1) for i in range(devices - 1)]
    backward = [(b, a) for a, b in forward]

    mine = conv_member(field, norm_gain[0, 0], conv_weight[0])
    split = mine.reshape(members, rows, devices, width, channels).transpose(2, 0, 1, 3, 4)
    arrived = lax.all_to_all(split, "mem", split_axis=0, concat_axis=0, tiled=True)
    state = arrived.reshape(all_members, rows * width, channels).transpose(1, 0, 2)
    state = attend(state, norm_gain[0, 1], qkv_weight[0], out_weight[0])
    for b in range(1, BLOCKS):
        grid = state.reshape(rows, width, all_members, channels)
        left = lax.ppermute(grid[:, -1:], "mem", forward)
        right = lax.ppermute(grid[:, :1], "mem", backward)
        grid = conv_cell(grid, left, right, norm_gain[b, 0], conv_weight[b])
        state = grid.reshape(rows * width, all_members, channels)
        state = attend(state, norm_gain[b, 1], qkv_weight[b], out_weight[b])
    back = state.transpose(1, 0, 2).reshape(devices, members, rows, width, channels)
    returned = lax.all_to_all(back, "mem", split_axis=0, concat_axis=0, tiled=True)
    return returned.transpose(1, 2, 0, 3, 4).reshape(members, rows, cols, channels)


def solution(mesh):
    return jax.shard_map(
        body,
        mesh=mesh,
        in_specs=(P(("grp", "mem"), None, None, None), P(), P(), P(), P()),
        out_specs=P(("grp", "mem"), None, None, None),
        check_vma=False,
    )
```

profile of v0, /device:TPU:0, one launch (start us, length us, event | category | flops | bytes accessed | tf_op | source)
XLA Modules:
  0.0 230.5 jit_solution(9304718505292399546)
XLA Ops:
  0.0 1.4 slice_bitcast_fusion.4
  1.4 4.9 %fusion.3 = (bf16[1,3,3,256,512]{4,3,2,1,0:T(8,128)(2,1)}, bf16[1,3,3,256,512]{4,3,2,1,0:T(8,128)(2,1)}) fusion(bf16[2,3,3,256,512]{4,3,2,1,0:T(8,128)(2,1)} %param.7), kind=kLoop, calls=%fused_computation.21 | loop fusion | bytes 9437184 | tf_op jit(solution)/shard_map/slice | solution.py:230
  6.3 13.9 %conv_member.1 = bf16[4,16,64,256]{3,2,1,0:T(8,128)(2,1)} custom-call(bf16[4,16,64,256]{3,2,1,0:T(8,128)(2,1)} %x_ref.1, f32[1,256]{1,0:T(1,128)} %get-tuple-element.15.gain_ref, bf16[3,768,512]{2,1,0:T(8,128)(2,1)} %bitcast.36), custom_call_target="tpu_custom_call" | custom-call | tf_op jit(solution)/shard_map/conv_member/pallas_call | solution.py:67
  20.2 2.5 %reshape.92 = bf16[4,16,16,4,256]{4,3,2,1,0:T(4,128)(2,1)S(1)} reshape(bf16[4,16,64,256]{3,2,1,0:T(8,128)(2,1)} %conv_member.1) | data formatting | bytes 4194304 | tf_op jit(solution)/shard_map/reshape | solution.py:222
  22.8 4.0 %copy.17 = bf16[4,16,16,4,256]{4,0,3,1,2:T(4,128)(2,1)} copy(bf16[4,16,16,4,256]{4,3,2,1,0:T(4,128)(2,1)S(1)} %reshape.92) | data formatting | bytes 4194304 | tf_op jit(solution)/shard_map/reshape | solution.py:222
  26.8 0.0 copy-start.3
  26.8 0.0 copy-start
  26.8 7.5 %all-to-all-start = ((bf16[16,4,16,4,256]{4,1,3,2,0:T(4,128)(2,1)}), bf16[16,4,16,4,256]{4,1,3,2,0:T(4,128)(2,1)S(1)}, u32[]{:S(2)}, u32[]{:S(2)}) async-start(bf16[16,4,16,4,256]{4,1,3,2,0:T(4,128)(2,1)} %bitcast.38), calls=%async_computation | async-start | bytes 4194304 | tf_op jit(solution)/shard_map/all_to_all | solution.py:223
  34.4 0.8 compare_convert_fusion.ones_ref
  35.2 0.0 copy-done.3
  35.2 0.7 slice_bitcast_fusion.2
  35.9 0.0 copy-done
  36.0 0.9 slice_bitcast_fusion
  36.9 38.4 %all-to-all-done = bf16[16,4,16,4,256]{4,1,3,2,0:T(4,128)(2,1)S(1)} async-done(((bf16[16,4,16,4,256]{4,1,3,2,0:T(4,128)(2,1)}), bf16[16,4,16,4,256]{4,1,3,2,0:T(4,128)(2,1)S(1)}, u32[]{:S(2)}, u32[]{:S(2)}) %all-to-all-start) | async-done | bytes 2097184 | tf_op jit(solution)/shard_map/all_to_all | solution.py:223
  75.3 2.5 %copy.12 = bf16[16,4,16,4,256]{4,1,0,3,2:T(4,128)(2,1)} copy(bf16[16,4,16,4,256]{4,1,3,2,0:T(4,128)(2,1)S(1)} %all-to-all-done) | data formatting | bytes 4194304 | tf_op jit(solution)/shard_map/all_to_all | solution.py:223
  77.8 4.0 %reshape.93 = bf16[64,64,256]{2,0,1:T(8,128)(2,1)} reshape(bf16[16,4,16,4,256]{4,1,0,3,2:T(4,128)(2,1)} %copy.12) | data formatting | bytes 4194304 | tf_op jit(solution)/shard_map/reshape | solution.py:224
  81.8 23.9 %attend.2 = bf16[64,64,256]{2,1,0:T(8,128)(2,1)} custom-call(bf16[64,64,256]{2,1,0:T(8,128)(2,1)} %bitcast.40, f32[1,256]{1,0:T(1,128)} %get-tuple-element.14.gain_ref, bf16[256,768]{1,0:T(8,128)(2,1)} %get-tuple-element.10.qkv_ref, bf16[256,256]{1,0:T(8,128)(2,1)} %get-tuple-element.12.out_w_ref, bf16[512,256]{1,0:T(8,128)(2,1)} %compare_convert_fusion.ones_ref), custom_call_target="tpu_custom_call" | custom-call | tf_op jit(solution)/shard_map/attend/pallas_call | solution.py:196
  105.7 1.3 fusion.4
  107.0 1.3 collective-permute-start.1
  108.3 3.7 %collective-permute-start = (bf16[16,1,64,256]{3,2,1,0:T(8,128)(2,1)S(1)}, bf16[16,1,64,256]{3,2,1,0:T(8,128)(2,1)S(1)}, u32[]{:S(2)}, u32[]{:S(2)}) collective-permute-start(bf16[16,1,64,256]{3,2,1,0:T(8,128)(2,1)S(1)} %get-tuple-element.8), channel_id=1, source_target_pairs={{0,1},{1,2},{2,3},{3,4},{4,5},{5,6},{6,7},{7,8},{8,9},{9,10},{10,1... | collective-permute-start | bytes 1572872 | tf_op jit(solution)/shard_map/ppermute | solution.py:228
  112.0 0.0 collective-permute-done.1.right_ref
  112.0 0.0 copy-start.1
  112.0 1.3 collective-permute-done.left_ref
  113.3 0.0 copy-done.1
  113.3 0.8 copy-done.2
  114.1 17.5 %conv_cell.1 = bf16[16,4,64,256]{3,2,1,0:T(8,128)(2,1)} custom-call(bf16[16,4,64,256]{3,2,1,0:T(8,128)(2,1)} %bitcast.35, bf16[16,1,64,256]{3,2,1,0:T(8,128)(2,1)} %copy-done.2, bf16[16,1,64,256]{3,2,1,0:T(8,128)(2,1)} %copy-done.1, f32[1,256]{1,0:T(1,128)} %get-tuple-element.16.gain_ref, bf16[3,768,512]{2,1,0:T(8,128)(2,1)} %bitcast.37), custom_call_target="tpu_custom_call" | custom-call | tf_op jit(solution)/shard_map/conv_cell/pallas_call | solution.py:123
  131.7 24.0 %attend.3 = bf16[64,64,256]{2,1,0:T(8,128)(2,1)} custom-call(bf16[64,64,256]{2,1,0:T(8,128)(2,1)} %bitcast.42, f32[1,256]{1,0:T(1,128)} %get-tuple-element.13.gain_ref, bf16[256,768]{1,0:T(8,128)(2,1)} %get-tuple-element.9.qkv_ref, bf16[256,256]{1,0:T(8,128)(2,1)} %get-tuple-element.11.out_w_ref, bf16[512,256]{1,0:T(8,128)(2,1)} %compare_convert_fusion.ones_ref), custom_call_target="tpu_custom_call" | custom-call | tf_op jit(solution)/shard_map/attend/pallas_call | solution.py:196
  155.6 2.5 %reshape.96 = bf16[16,4,16,4,256]{4,1,0,3,2:T(4,128)(2,1)S(1)} reshape(bf16[64,64,256]{2,0,1:T(8,128)(2,1)} %bitcast.39) | data formatting | bytes 4194304 | tf_op jit(solution)/shard_map/reshape | solution.py:233
  158.2 1.0 copy.13
  159.1 68.6 %all_to_all.10 = bf16[16,4,16,4,256]{4,1,3,2,0:T(4,128)(2,1)S(1)} all-to-all(bf16[16,4,16,4,256]{4,1,3,2,0:T(4,128)(2,1)S(1)} %copy.13), channel_id=1, replica_groups=mesh['grp'=2,'mem'=16] {'mem'}, dimensions={0} | all-to-all | bytes 4194304 | tf_op jit(solution)/shard_map/all_to_all | solution.py:234
  227.7 0.7 copy.14
  228.5 2.1 copy.15
  (3 shorter events, 0.0 us)
Async XLA Ops:
  26.8 8.4 %copy-start.3 = (bf16[2,256,256]{2,1,0:T(8,128)(2,1)S(1)}, bf16[2,256,256]{2,1,0:T(8,128)(2,1)}, u32[]{:S(2)}) copy-start(bf16[2,256,256]{2,1,0:T(8,128)(2,1)} %param.9) | copy-start | bytes 786436
  26.8 9.2 %copy-start = (bf16[2,256,768]{2,1,0:T(8,128)(2,1)S(1)}, bf16[2,256,768]{2,1,0:T(8,128)(2,1)}, u32[]{:S(2)}) copy-start(bf16[2,256,768]{2,1,0:T(8,128)(2,1)} %param.8) | copy-start | bytes 2359300
  26.8 48.5 %all-to-all-start = ((bf16[16,4,16,4,256]{4,1,3,2,0:T(4,128)(2,1)}), bf16[16,4,16,4,256]{4,1,3,2,0:T(4,128)(2,1)S(1)}, u32[]{:S(2)}, u32[]{:S(2)}) async-start(bf16[16,4,16,4,256]{4,1,3,2,0:T(4,128)(2,1)} %bitcast.38), calls=%async_computation | async-start | bytes 4194304 | tf_op jit(solution)/shard_map/all_to_all | solution.py:223
  107.0 5.0 %collective-permute-start.1 = (bf16[16,1,64,256]{3,2,1,0:T(8,128)(2,1)S(1)}, bf16[16,1,64,256]{3,2,1,0:T(8,128)(2,1)S(1)}, u32[]{:S(2)}, u32[]{:S(2)}) collective-permute-start(bf16[16,1,64,256]{3,2,1,0:T(8,128)(2,1)S(1)} %get-tuple-element.7), channel_id=1, source_target_pairs={{1,0},{2,1},{3,2},{4,3},{5,4},{6,5},{7,6},{8,7},{9,8},{10,9},{11,1... | collective-permute-start | bytes 1572872 | tf_op jit(solution)/shard_map/ppermute | solution.py:229
  108.3 5.0 %collective-permute-start = (bf16[16,1,64,256]{3,2,1,0:T(8,128)(2,1)S(1)}, bf16[16,1,64,256]{3,2,1,0:T(8,128)(2,1)S(1)}, u32[]{:S(2)}, u32[]{:S(2)}) collective-permute-start(bf16[16,1,64,256]{3,2,1,0:T(8,128)(2,1)S(1)} %get-tuple-element.8), channel_id=1, source_target_pairs={{0,1},{1,2},{2,3},{3,4},{4,5},{5,6},{6,7},{7,8},{8,9},{9,10},{10,1... | collective-permute-start | bytes 1572872 | tf_op jit(solution)/shard_map/ppermute | solution.py:228
  112.0 1.3 copy-start.1
  113.3 0.8 copy-start.2
where the time goes:
time: 232 us; the launch traced here: 231 us
  Pallas kernels  79.4 us (34%)
  blocking collectives  68.6 us (30%)
  waiting for transfers between devices  39.7 us (17%)
  local copies, waits for them, and re-layouts  29.4 us (13%)
  starting transfers between devices  12.6 us (5%)
    all_to_all x1, blocking collectives, body(): lax.all_to_all(back, 'mem', split_axis=0, concat_axis=0, tiled=True)  68.6 us
    pallas_call x2, Pallas kernels, attend(): pl.pallas_call(attend_kernel, grid=(cells // block,), in_specs=[spec, pl....  47.9 us
    all_to_all x1, waiting for transfers between devices, body(): lax.all_to_all(split, 'mem', split_axis=0, concat_axis=0, tiled=True)  38.4 us
    pallas_call x1, Pallas kernels, conv_cell(): pl.pallas_call(conv_cell_kernel, in_specs=[pl.BlockSpec(memory_space=pltp...  17.5 us
    pallas_call x1, Pallas kernels, conv_member(): pl.pallas_call(conv_member_kernel, grid=(members,), in_specs=[pl.BlockSpe...  13.9 us
    all_to_all x1, starting transfers between devices, body(): lax.all_to_all(split, 'mem', split_axis=0, concat_axis=0, tiled=True)  7.55 us
    reshape x2, local copies, waits for them, and re-layouts, body(): mine.reshape(members, rows, devices, width, channels)  6.56 us
    slice x1, local copies, waits for them, and re-layouts, body(): grid = conv_cell(grid, left, right, norm_gain[b, 0], conv_weight[b])  4.91 us
  transfers between devices with their start and end apart: 3, of which 2 were waited for; matrix products, arithmetic and copies ran while one was open for 1% of the time, Pallas kernels for 0%

commit v1 on v0

v1 whole, which is shorter than its diff:
```python
import functools

import jax
import jax.numpy as jnp
from jax import lax
from jax.experimental import pallas as pl
from jax.experimental.pallas import tpu as pltpu
from jax.sharding import PartitionSpec as P

HEADS = 8
epsilon = 1e-06
VMEM_LIMIT = 58 * 1024 * 1024


def normalised(x, gain):
    inverse = lax.rsqrt(jnp.mean(x * x, axis=-1, keepdims=True) + epsilon)
    return x * inverse * gain


def gated(x, conv_out):
    channels = x.shape[-1]
    gate = conv_out[:, channels:]
    return x + conv_out[:, :channels] * (1.0 / (1.0 + jnp.exp(-gate)))


def taps(wide_ref, weight_ref, row, step):
    total = None
    for di in range(3):
        lhs = wide_ref[pl.ds(row + di, step)]
        lhs = lhs.reshape(-1, lhs.shape[-1])
        part = jnp.dot(lhs, weight_ref[di], preferred_element_type=jnp.float32)
        total = part if total is None else total + part
    return total


def conv_cell_kernel(x_ref, left_ref, right_ref, gain_ref, weight_ref, out_ref, wide_ref):
    rows, cols, members, channels = x_ref.shape
    gain = gain_ref[...]
    zero = jnp.zeros((1, cols, members, 3 * channels), jnp.bfloat16)
    wide_ref[0:1] = zero
    wide_ref[rows + 1 : rows + 2] = zero

    @pl.loop(0, rows)
    def _(row):
        def normed_of(ref, col):
            x = ref[row, col].astype(jnp.float32)
            return normalised(x, gain).astype(jnp.bfloat16)

        for col in range(-1, cols + 1):
            if col < 0:
                value = normed_of(left_ref, 0)
            elif col == cols:
                value = normed_of(right_ref, 0)
            else:
                value = normed_of(x_ref, col)
            for dj in range(3):
                target = col + 1 - dj
                if 0 <= target < cols:
                    wide_ref[row + 1, target, :, dj * channels : (dj + 1) * channels] = value

    step = max(1, min(rows, 512 // (cols * members)))

    @pl.loop(0, rows // step)
    def _(index):
        row = index * step
        conv_out = taps(wide_ref, weight_ref, row, step)
        x = x_ref[pl.ds(row, step)].astype(jnp.float32).reshape(-1, channels)
        out_ref[pl.ds(row, step)] = (
            gated(x, conv_out).astype(jnp.bfloat16).reshape(step, cols, members, channels)
        )


def conv_cell(state, left, right, gain_row, weight):
    rows, cols, members, channels = state.shape
    weight = weight.reshape(3, 3 * channels, 2 * channels)
    return pl.pallas_call(
        conv_cell_kernel,
        in_specs=[pl.BlockSpec(memory_space=pltpu.VMEM)] * 5,
        out_specs=pl.BlockSpec(memory_space=pltpu.VMEM),
        out_shape=jax.ShapeDtypeStruct(state.shape, jnp.bfloat16),
        scratch_shapes=[pltpu.VMEM((rows + 2, cols, members, 3 * channels), jnp.bfloat16)],
        compiler_params=pltpu.CompilerParams(vmem_limit_bytes=VMEM_LIMIT),
        name="conv_cell",
    )(state, left, right, gain_row.reshape(1, channels), weight)


def attend_block(x, gain, qkv_ref, out_w_ref, ones_ref):
    cells, members, channels = x.shape
    head_size = channels // HEADS
    scale = head_size ** (-0.5)
    rows = x.reshape(cells * members, channels)
    normed = normalised(rows, gain).astype(jnp.bfloat16)
    projected = jnp.dot(normed, qkv_ref[...], preferred_element_type=jnp.float32).astype(
        jnp.bfloat16
    )
    lane_head = lax.broadcasted_iota(jnp.int32, (members, channels), 1) // head_size
    masks = [lane_head == h for h in range(HEADS)]
    zero = jnp.zeros((members, channels), jnp.bfloat16)
    per = max(1, 128 // members)
    width = per * members
    lane_slot = lax.broadcasted_iota(jnp.int32, (members, width), 1) // members
    weights, mixed = [], []
    for cell in range(cells):
        block = projected[cell * members : (cell + 1) * members]
        queries = block[:, :channels]
        keys = block[:, channels : 2 * channels]
        values = block[:, 2 * channels :]
        spread_keys = jnp.concatenate([jnp.where(m, keys, zero) for m in masks], axis=0)
        spread_values = jnp.concatenate([jnp.where(m, values, zero) for m in masks], axis=0)
        scores = lax.dot_general(
            queries, spread_keys, (((1,), (1,)), ((), ())), preferred_element_type=jnp.float32
        )
        parts = []
        for tile in range(HEADS // per):
            s = scores[:, tile * width : (tile + 1) * width]
            if per == 1:
                most = jnp.max(s, axis=-1, keepdims=True)
            else:
                most = jnp.zeros_like(s)
                for slot in range(per):
                    here = lane_slot == slot
                    top = jnp.max(jnp.where(here, s, -jnp.inf), axis=-1, keepdims=True)
                    most = jnp.where(here, top, most)
            parts.append(jnp.exp((s - most) * scale).astype(jnp.bfloat16))
        weight = jnp.concatenate(parts, axis=1)
        weights.append(weight)
        mixed.append(jnp.dot(weight, spread_values, preferred_element_type=jnp.float32))
    weight = jnp.concatenate(weights, axis=0)
    total = jnp.dot(weight, ones_ref[...], preferred_element_type=jnp.float32)
    attended = (jnp.concatenate(mixed, axis=0) / total).astype(jnp.bfloat16)
    update = jnp.dot(attended, out_w_ref[...], preferred_element_type=jnp.float32)
    return (rows + update).reshape(x.shape)


def head_sums(members, channels):
    row = jnp.arange(HEADS * members)[:, None] // members
    lane = jnp.arange(channels)[None, :] // (channels // HEADS)
    return (row == lane).astype(jnp.bfloat16)


def enter(devices, me):
    barrier = pltpu.get_barrier_semaphore()

    @pl.loop(1, devices)
    def _(k):
        pl.semaphore_signal(
            barrier,
            inc=1,
            device_id={"mem": lax.rem(me + k, devices)},
            device_id_type=pl.DeviceIdType.MESH,
        )

    pl.semaphore_wait(barrier, devices - 1)


def exchange(source_of, target, me, devices, send_sem, recv_sem):
    own = pltpu.make_async_copy(source_of(me), target, recv_sem.at[me])
    own.start()

    @pl.loop(1, devices)
    def _(k):
        to = lax.rem(me + k, devices)
        pltpu.make_async_remote_copy(
            src_ref=source_of(to),
            dst_ref=target,
            send_sem=send_sem.at[to],
            recv_sem=recv_sem.at[me],
            device_id={"mem": to},
            device_id_type=pl.DeviceIdType.MESH,
        ).start()


def wait_all(ref, me, devices, sem, own):
    @pl.loop(0 if own else 1, devices)
    def _(k):
        pltpu.make_async_copy(ref, ref, sem.at[lax.rem(me + k, devices)]).wait()


def swap_strips(parts, width):
    count = len(parts)
    slot = lax.broadcasted_iota(jnp.int32, parts[0].shape, parts[0].ndim - 2) // width
    results = []
    for j in range(count):
        total = None
        for i in range(count):
            shift = ((i - j) * width) % (count * width)
            part = parts[i] if shift == 0 else pltpu.roll(parts[i], shift, parts[i].ndim - 2)
            total = part if total is None else jnp.where(slot == i, part, total)
        results.append(total)
    return results


def first_kernel(
    devices,
    x_ref,
    gain_ref,
    conv_ref,
    gain2_ref,
    qkv_ref,
    out_w_ref,
    ones_ref,
    out_ref,
    wide_ref,
    send_ref,
    recv_ref,
    send_sem,
    recv_sem,
):
    members, rows, cols, channels = x_ref.shape
    width = cols // devices
    batch = 8 // width
    chunks = rows // batch
    groups = cols // 8
    me = lax.axis_index("mem")
    gain = gain_ref[...]
    flat = batch * cols
    column = lax.broadcasted_iota(jnp.int32, (flat, channels), 0) % cols

    def fill(row):
        for member in range(members):
            x = x_ref[member, pl.ds(row, batch)].astype(jnp.float32).reshape(flat, channels)
            normed = normalised(x, gain)
            left = jnp.where(column == 0, 0.0, pltpu.roll(normed, 1, 0))
            right = jnp.where(column == cols - 1, 0.0, pltpu.roll(normed, flat - 1, 0))
            for at, value in enumerate((left, normed, right)):
                wide_ref[
                    member, pl.ds(row + 1, batch), :, at * channels : (at + 1) * channels
                ] = value.astype(jnp.bfloat16).reshape(batch, cols, channels)

    zero = jnp.zeros((members, 1, cols, 3 * channels), jnp.bfloat16)
    wide_ref[:, 0:1] = zero
    wide_ref[:, rows + 1 : rows + 2] = zero
    fill(0)
    enter(devices, me)

    @pl.loop(0, chunks)
    def _(q):
        row = q * batch

        @pl.when(q < chunks - 1)
        def _():
            fill(row + batch)

        total = None
        for di in range(3):
            lhs = wide_ref[:, pl.ds(row + di, batch)].reshape(members * flat, 3 * channels)
            part = jnp.dot(lhs, conv_ref[di], preferred_element_type=jnp.float32)
            total = part if total is None else total + part
        x = x_ref[:, pl.ds(row, batch)].astype(jnp.float32).reshape(members * flat, channels)
        y = gated(x, total).reshape(members, batch, groups, 8, channels)
        parts = swap_strips(
            [y[:, i].reshape(members * groups, 8, channels) for i in range(batch)], width
        )
        for j in range(batch):
            part = parts[j].astype(jnp.bfloat16).reshape(members, groups, 8, channels)
            for k in range(groups):
                send_ref[q, k * batch + j] = part[:, k]
        exchange(
            lambda d: send_ref.at[q, d],
            recv_ref.at[q, me],
            me,
            devices,
            send_sem.at[q],
            recv_sem.at[q],
        )

    @pl.loop(0, chunks)
    def _(q):
        wait_all(recv_ref.at[q, 0], me, devices, recv_sem.at[q], True)
        x = recv_ref[q].astype(jnp.float32).reshape(devices * members, 8, channels)
        x = jnp.transpose(x, (1, 0, 2))
        y = attend_block(x, gain2_ref[...], qkv_ref, out_w_ref, ones_ref)
        out_ref[pl.ds(q * 8, 8)] = y.astype(jnp.bfloat16)

    @pl.loop(0, chunks)
    def _(q):
        wait_all(send_ref.at[q, 0], me, devices, send_sem.at[q], False)


def last_kernel(
    devices,
    x_ref,
    gain2_ref,
    qkv_ref,
    out_w_ref,
    ones_ref,
    out_ref,
    send_ref,
    recv_ref,
    send_sem,
    recv_sem,
):
    members, rows, cols, channels = out_ref.shape
    width = cols // devices
    batch = 8 // width
    chunks = rows // batch
    groups = cols // 8
    me = lax.axis_index("mem")
    enter(devices, me)

    @pl.loop(0, chunks)
    def _(q):
        x = x_ref[pl.ds(q * 8, 8)].astype(jnp.float32)
        y = attend_block(x, gain2_ref[...], qkv_ref, out_w_ref, ones_ref)
        y = jnp.transpose(y, (1, 0, 2)).astype(jnp.bfloat16)
        send_ref[q] = y.reshape(devices, members, 8, channels)
        exchange(
            lambda d: send_ref.at[q, d],
            recv_ref.at[q, me],
            me,
            devices,
            send_sem.at[q],
            recv_sem.at[q],
        )

    @pl.loop(0, chunks)
    def _(q):
        wait_all(recv_ref.at[q, 0], me, devices, recv_sem.at[q], True)
        parts = []
        for j in range(batch):
            part = [recv_ref[q, k * batch + j].astype(jnp.float32) for k in range(groups)]
            parts.append(jnp.concatenate(part, axis=0))
        for i, part in enumerate(swap_strips(parts, width)):
            part = part.reshape(groups, members, 8, channels)
            for member in range(members):
                line = jnp.concatenate([part[k, member] for k in range(groups)], axis=0)
                out_ref[member, q * batch + i] = line.astype(jnp.bfloat16)

    @pl.loop(0, chunks)
    def _(q):
        wait_all(send_ref.at[q, 0], me, devices, send_sem.at[q], False)


def whole(count):
    return [pl.BlockSpec(memory_space=pltpu.VMEM)] * count


def transfers(chunks, devices, members, channels):
    block = pltpu.VMEM((chunks, devices, members, 8, channels), jnp.bfloat16)
    sems = pltpu.SemaphoreType.DMA((chunks, devices))
    return [block, block, sems, sems]


def first(field, gain, weight, gain2, qkv, out_w, devices):
    members, rows, cols, channels = field.shape
    batch = 8 // (cols // devices)
    cells = rows * cols // devices
    shape = (cells, members * devices, channels)
    return pl.pallas_call(
        functools.partial(first_kernel, devices),
        in_specs=whole(7),
        out_specs=pl.BlockSpec(memory_space=pltpu.VMEM),
        out_shape=jax.ShapeDtypeStruct(shape, jnp.bfloat16),
        scratch_shapes=[
            pltpu.VMEM((members, rows + 2, cols, 3 * channels), jnp.bfloat16),
            *transfers(rows // batch, devices, members, channels),
        ],
        compiler_params=pltpu.CompilerParams(
            vmem_limit_bytes=VMEM_LIMIT, collective_id=0, has_side_effects=True
        ),
        name="conv_scatter_attend",
    )(
        field,
        gain.reshape(1, channels),
        weight.reshape(3, 3 * channels, 2 * channels),
        gain2.reshape(1, channels),
        qkv,
        out_w,
        head_sums(members * devices, channels),
    )


def last(state, gain2, qkv, out_w, shape, devices):
    members, rows, cols, channels = shape
    batch = 8 // (cols // devices)
    return pl.pallas_call(
        functools.partial(last_kernel, devices),
        in_specs=whole(5),
        out_specs=pl.BlockSpec(memory_space=pltpu.VMEM),
        out_shape=jax.ShapeDtypeStruct(shape, jnp.bfloat16),
        scratch_shapes=transfers(rows // batch, devices, members, channels),
        compiler_params=pltpu.CompilerParams(
            vmem_limit_bytes=VMEM_LIMIT, collective_id=1, has_side_effects=True
        ),
        name="attend_gather",
    )(
        state,
        gain2.reshape(1, channels),
        qkv,
        out_w,
        head_sums(members * devices, channels),
    )


def body(field, norm_gain, conv_weight, qkv_weight, out_weight):
    members, rows, cols, channels = field.shape
    devices = lax.axis_size("mem")
    width = cols // devices
    forward = [(i, i + 1) for i in range(devices - 1)]
    backward = [(b, a) for a, b in forward]
    state = first(
        field, norm_gain[0, 0], conv_weight[0], norm_gain[0, 1], qkv_weight[0], out_weight[0], devices
    )
    grid = state.reshape(rows, width, members * devices, channels)
    left = lax.ppermute(grid[:, -1:], "mem", forward)
    right = lax.ppermute(grid[:, :1], "mem", backward)
    grid = conv_cell(grid, left, right, norm_gain[1, 0], conv_weight[1])
    state = grid.reshape(state.shape)
    return last(state, norm_gain[1, 1], qkv_weight[1], out_weight[1], field.shape, devices)


def solution(mesh):
    return jax.shard_map(
        body,
        mesh=mesh,
        in_specs=(P(("grp", "mem"), None, None, None), P(), P(), P(), P()),
        out_specs=P(("grp", "mem"), None, None, None),
        check_vma=False,
    )
```

time: 232 us -> 173 us (0.75)
  Pallas kernels: 79.4 us -> 151 us
  blocking collectives: 68.6 us -> 0 us
  waiting for transfers between devices: 39.7 us -> 1.47 us
  local copies, waits for them, and re-layouts: 29.4 us -> 15.2 us
  starting transfers between devices: 12.6 us -> 4.36 us
    pallas_call x3 -> x2, Pallas kernels: 61.8 us -> 133 us  [the longest x1 70.3 us: last(): pl.pallas_call(functools.partial(last_kernel, devices), in_specs=whole(5)...]
    all_to_all x1 -> x0, blocking collectives: 68.6 us -> none  [body(): lax.all_to_all(back, 'mem', split_axis=0, concat_axis=0, tiled=True)]
    all_to_all x1 -> x0, waiting for transfers between devices: 38.4 us -> none  [body(): lax.all_to_all(split, 'mem', split_axis=0, concat_axis=0, tiled=True)]
    reshape x6 -> x0, local copies, waits for them, and re-layouts: 16.1 us -> none  [the longest x2 6.56 us: body(): mine.reshape(members, rows, devices, width, channels)]
    all_to_all x1 -> x0, starting transfers between devices: 7.55 us -> none  [body(): lax.all_to_all(split, 'mem', split_axis=0, concat_axis=0, tiled=True)]
    all_to_all x2 -> x0, local copies, waits for them, and re-layouts: 3.19 us -> none  [the longest x1 2.48 us: body(): lax.all_to_all(split, 'mem', split_axis=0, concat_axis=0, tiled=True)]
    unnamed x8 -> x5, local copies, waits for them, and re-layouts: 0.82 us -> 3.96 us
  transfers between devices with their start and end apart: 3 -> 2, of which waited for: 2 -> 1; matrix products, arithmetic and copies ran while one was open for 1% -> 0% of each run, Pallas kernels for 0% -> 0%
where the time goes in v1:
time: 173 us
  Pallas kernels  151 us (87%)
  local copies, waits for them, and re-layouts  15.2 us (9%)
  starting transfers between devices  4.36 us (3%)
    pallas_call x1, Pallas kernels, last(): pl.pallas_call(functools.partial(last_kernel, devices), in_specs=whole(5)...  70.3 us
    pallas_call x1, Pallas kernels, first(): pl.pallas_call(functools.partial(first_kernel, devices), in_specs=whole(7...  62.9 us
    pallas_call x1, Pallas kernels, conv_cell(): pl.pallas_call(conv_cell_kernel, in_specs=[pl.BlockSpec(memory_space=pltp...  17.6 us
    slice x1, local copies, waits for them, and re-layouts, body(): grid = conv_cell(grid, left, right, norm_gain[1, 0], conv_weight[1])  4.91 us
    unnamed x5, local copies, waits for them, and re-layouts  3.96 us
  transfers between devices with their start and end apart: 2, of which 1 were waited for; matrix products, arithmetic and copies ran while one was open for 0% of the time, Pallas kernels for 0%

profile of v1, /device:TPU:0, one launch (start us, length us, event | category | flops | bytes accessed | tf_op | source)
XLA Modules:
  0.0 172.8 jit_solution(11078843920018352908)
XLA Ops:
  0.0 1.4 slice_bitcast_fusion.4
  1.4 1.7 slice_bitcast_fusion.2
  3.0 2.0 %slice_bitcast_fusion = (bf16[256,768]{1,0:T(8,128)(2,1)}, bf16[256,768]{1,0:T(8,128)(2,1)}) fusion(bf16[2,256,768]{2,1,0:T(8,128)(2,1)} %param.8), kind=kLoop, calls=%fused_computation.1 | loop fusion | bytes 1572864 | tf_op jit(solution)/shard_map/squeeze | solution.py:409
  5.1 4.9 %fusion.3 = (bf16[1,3,3,256,512]{4,3,2,1,0:T(8,128)(2,1)}, bf16[1,3,3,256,512]{4,3,2,1,0:T(8,128)(2,1)}) fusion(bf16[2,3,3,256,512]{4,3,2,1,0:T(8,128)(2,1)} %param.7), kind=kLoop, calls=%fused_computation.20 | loop fusion | bytes 9437184 | tf_op jit(solution)/shard_map/slice | solution.py:407
  10.0 0.8 compare_convert_fusion.ones_ref
  10.8 62.9 %conv_scatter_attend.1 = bf16[64,64,256]{2,1,0:T(8,128)(2,1)} custom-call(bf16[4,16,64,256]{3,2,1,0:T(8,128)(2,1)} %x_ref.1, f32[1,256]{1,0:T(1,128)} %get-tuple-element.15.gain_ref, bf16[3,768,512]{2,1,0:T(8,128)(2,1)} %bitcast.23, f32[1,256]{1,0:T(1,128)} %get-tuple-element.14.gain2_ref, bf16[256,768]{1,0:T(8,128)(2,1)} %get-tuple-element.10.qkv_ref, ...), custom_call_target="tpu_custom_call" | custom-call | tf_op jit(solution)/shard_map/conv_scatter_attend/pallas_call | solution.py:349
  73.8 1.3 fusion.4
  75.1 1.3 collective-permute-start.1
  76.4 3.1 %collective-permute-start = (bf16[16,1,64,256]{3,2,1,0:T(8,128)(2,1)S(1)}, bf16[16,1,64,256]{3,2,1,0:T(8,128)(2,1)S(1)}, u32[]{:S(2)}, u32[]{:S(2)}) collective-permute-start(bf16[16,1,64,256]{3,2,1,0:T(8,128)(2,1)S(1)} %get-tuple-element.8), channel_id=1, source_target_pairs={{0,1},{1,2},{2,3},{3,4},{4,5},{5,6},{6,7},{7,8},{8,9},{9,10},{10,1... | collective-permute-start | bytes 1572872 | tf_op jit(solution)/shard_map/ppermute | solution.py:405
  79.4 0.0 collective-permute-done.1.right_ref
  79.4 0.0 copy-start
  79.4 1.5 collective-permute-done.left_ref
  80.9 0.0 copy-start.1
  80.9 0.0 copy-done
  80.9 0.8 copy-done.1
  81.7 17.6 %conv_cell.1 = bf16[16,4,64,256]{3,2,1,0:T(8,128)(2,1)} custom-call(bf16[16,4,64,256]{3,2,1,0:T(8,128)(2,1)} %bitcast.21, bf16[16,1,64,256]{3,2,1,0:T(8,128)(2,1)} %copy-done.1, bf16[16,1,64,256]{3,2,1,0:T(8,128)(2,1)} %copy-done, f32[1,256]{1,0:T(1,128)} %get-tuple-element.16.gain_ref, bf16[3,768,512]{2,1,0:T(8,128)(2,1)} %bitcast.22), custom_call_target="tpu_custom_call" | custom-call | tf_op jit(solution)/shard_map/conv_cell/pallas_call | solution.py:76
  99.3 70.3 %attend_gather.1 = bf16[4,16,64,256]{3,2,1,0:T(8,128)(2,1)} custom-call(bf16[64,64,256]{2,1,0:T(8,128)(2,1)} %bitcast.24, f32[1,256]{1,0:T(1,128)} %get-tuple-element.13.gain2_ref, bf16[256,768]{1,0:T(8,128)(2,1)} %get-tuple-element.9.qkv_ref, bf16[256,256]{1,0:T(8,128)(2,1)} %get-tuple-element.11.out_w_ref, bf16[512,256]{1,0:T(8,128)(2,1)} %compare_convert_fusion.ones_ref), custom_call_target="tpu_custom_call" | custom-call | tf_op jit(solution)/shard_map/attend_gather/pallas_call | solution.py:376
  169.6 3.2 %copy.7 = bf16[4,16,64,256]{3,2,1,0:T(8,128)(2,1)} copy(bf16[4,16,64,256]{3,2,1,0:T(8,128)(2,1)} %attend_gather.1) | data formatting | bytes 4194304
  (2 shorter events, 0.0 us)
Async XLA Ops:
  75.1 4.4 %collective-permute-start.1 = (bf16[16,1,64,256]{3,2,1,0:T(8,128)(2,1)S(1)}, bf16[16,1,64,256]{3,2,1,0:T(8,128)(2,1)S(1)}, u32[]{:S(2)}, u32[]{:S(2)}) collective-permute-start(bf16[16,1,64,256]{3,2,1,0:T(8,128)(2,1)S(1)} %get-tuple-element.7), channel_id=1, source_target_pairs={{1,0},{2,1},{3,2},{4,3},{5,4},{6,5},{7,6},{8,7},{9,8},{10,9},{11,1... | collective-permute-start | bytes 1572872 | tf_op jit(solution)/shard_map/ppermute | solution.py:406
  76.4 4.6 %collective-permute-start = (bf16[16,1,64,256]{3,2,1,0:T(8,128)(2,1)S(1)}, bf16[16,1,64,256]{3,2,1,0:T(8,128)(2,1)S(1)}, u32[]{:S(2)}, u32[]{:S(2)}) collective-permute-start(bf16[16,1,64,256]{3,2,1,0:T(8,128)(2,1)S(1)} %get-tuple-element.8), channel_id=1, source_target_pairs={{0,1},{1,2},{2,3},{3,4},{4,5},{5,6},{6,7},{7,8},{8,9},{9,10},{10,1... | collective-permute-start | bytes 1572872 | tf_op jit(solution)/shard_map/ppermute | solution.py:405
  79.4 1.5 copy-start
  80.9 0.8 copy-start.1

commit v2 on v1

v2 whole, which is shorter than its diff:
```python
import functools

import jax
import jax.numpy as jnp
from jax import lax
from jax.experimental import pallas as pl
from jax.experimental.pallas import tpu as pltpu
from jax.sharding import PartitionSpec as P

HEADS = 8
epsilon = 1e-06
VMEM_LIMIT = 58 * 1024 * 1024


def normalised(x, gain):
    inverse = lax.rsqrt(jnp.mean(x * x, axis=-1, keepdims=True) + epsilon)
    return x * inverse * gain


def gated(x, conv_out):
    channels = x.shape[-1]
    gate = conv_out[:, channels:]
    return x + conv_out[:, :channels] * (1.0 / (1.0 + jnp.exp(-gate)))


def taps(rows_of, weight_ref):
    total = None
    for di in range(3):
        lhs = rows_of(di)
        lhs = lhs.reshape(-1, lhs.shape[-1])
        weight = weight_ref[di].reshape(lhs.shape[-1], -1)
        part = jnp.dot(lhs, weight, preferred_element_type=jnp.float32)
        total = part if total is None else total + part
    return total


def attend_block(x, gain, qkv, out_w, ones_ref):
    cells, members, channels = x.shape
    head_size = channels // HEADS
    scale = head_size ** (-0.5)
    rows = x.reshape(cells * members, channels)
    normed = normalised(rows, gain).astype(jnp.bfloat16)
    projected = jnp.dot(normed, qkv, preferred_element_type=jnp.float32).astype(
        jnp.bfloat16
    )
    lane_head = lax.broadcasted_iota(jnp.int32, (members, channels), 1) // head_size
    masks = [lane_head == h for h in range(HEADS)]
    zero = jnp.zeros((members, channels), jnp.bfloat16)
    per = max(1, 128 // members)
    width = per * members
    lane_slot = lax.broadcasted_iota(jnp.int32, (members, width), 1) // members
    weights, mixed = [], []
    for cell in range(cells):
        block = projected[cell * members : (cell + 1) * members]
        queries = block[:, :channels]
        keys = block[:, channels : 2 * channels]
        values = block[:, 2 * channels :]
        spread_keys = jnp.concatenate([jnp.where(m, keys, zero) for m in masks], axis=0)
        spread_values = jnp.concatenate([jnp.where(m, values, zero) for m in masks], axis=0)
        scores = lax.dot_general(
            queries, spread_keys, (((1,), (1,)), ((), ())), preferred_element_type=jnp.float32
        )
        parts = []
        for tile in range(HEADS // per):
            s = scores[:, tile * width : (tile + 1) * width]
            if per == 1:
                most = jnp.max(s, axis=-1, keepdims=True)
            else:
                most = jnp.zeros_like(s)
                for slot in range(per):
                    here = lane_slot == slot
                    top = jnp.max(jnp.where(here, s, -jnp.inf), axis=-1, keepdims=True)
                    most = jnp.where(here, top, most)
            parts.append(jnp.exp((s - most) * scale).astype(jnp.bfloat16))
        weight = jnp.concatenate(parts, axis=1)
        weights.append(weight)
        mixed.append(jnp.dot(weight, spread_values, preferred_element_type=jnp.float32))
    weight = jnp.concatenate(weights, axis=0)
    total = jnp.dot(weight, ones_ref[...], preferred_element_type=jnp.float32)
    attended = (jnp.concatenate(mixed, axis=0) / total).astype(jnp.bfloat16)
    update = jnp.dot(attended, out_w, preferred_element_type=jnp.float32)
    return (rows + update).reshape(x.shape)


def enter(devices, me):
    barrier = pltpu.get_barrier_semaphore()

    @pl.loop(1, devices)
    def _(k):
        pl.semaphore_signal(
            barrier,
            inc=1,
            device_id={"mem": lax.rem(me + k, devices)},
            device_id_type=pl.DeviceIdType.MESH,
        )

    pl.semaphore_wait(barrier, devices - 1)


def exchange(source_of, target, me, devices, send_sem, recv_sem):
    own = pltpu.make_async_copy(source_of(me), target, recv_sem.at[me])
    own.start()

    @pl.loop(1, devices)
    def _(k):
        to = lax.rem(me + k, devices)
        pltpu.make_async_remote_copy(
            src_ref=source_of(to),
            dst_ref=target,
            send_sem=send_sem.at[to],
            recv_sem=recv_sem.at[me],
            device_id={"mem": to},
            device_id_type=pl.DeviceIdType.MESH,
        ).start()


def wait_all(ref, me, devices, sem, own):
    @pl.loop(0 if own else 1, devices)
    def _(k):
        pltpu.make_async_copy(ref, ref, sem.at[lax.rem(me + k, devices)]).wait()


def swap_strips(parts, width):
    count = len(parts)
    slot = lax.broadcasted_iota(jnp.int32, parts[0].shape, parts[0].ndim - 2) // width
    results = []
    for j in range(count):
        total = None
        for i in range(count):
            shift = ((i - j) * width) % (count * width)
            part = parts[i] if shift == 0 else pltpu.roll(parts[i], shift, parts[i].ndim - 2)
            total = part if total is None else jnp.where(slot == i, part, total)
        results.append(total)
    return results


def kernel(
    devices,
    x_ref,
    gain_ref,
    conv_hbm,
    qkv_ref,
    out_w_ref,
    out_ref,
    conv_ref,
    ones_ref,
    wide_ref,
    wide2_ref,
    state_ref,
    left_ref,
    right_ref,
    send_ref,
    recv_ref,
    send2_ref,
    recv2_ref,
    conv_sem,
    send_sem,
    recv_sem,
    send2_sem,
    recv2_sem,
    edge_send,
    edge_recv,
):
    members, rows, cols, channels = x_ref.shape
    width = cols // devices
    batch = 8 // width
    chunks = rows // batch
    groups = cols // 8
    everyone = members * devices
    me = lax.axis_index("mem")
    flat = batch * cols
    column = lax.broadcasted_iota(jnp.int32, (flat, channels), 0) % cols
    loads = [
        pltpu.make_async_copy(conv_hbm.at[b], conv_ref.at[b], conv_sem.at[b]) for b in range(2)
    ]
    for load in loads:
        load.start()

    def fill(row):
        for member in range(members):
            x = x_ref[member, pl.ds(row, batch)].astype(jnp.float32).reshape(flat, channels)
            normed = normalised(x, gain_ref[0, 0:1])
            left = jnp.where(column == 0, 0.0, pltpu.roll(normed, 1, 0))
            right = jnp.where(column == cols - 1, 0.0, pltpu.roll(normed, flat - 1, 0))
            for at, value in enumerate((left, normed, right)):
                wide_ref[
                    member, pl.ds(row + 1, batch), :, at * channels : (at + 1) * channels
                ] = value.astype(jnp.bfloat16).reshape(batch, cols, channels)

    zero = jnp.zeros((members, 1, cols, 3 * channels), jnp.bfloat16)
    wide_ref[:, 0:1] = zero
    wide_ref[:, rows + 1 : rows + 2] = zero
    fill(0)
    enter(devices, me)
    loads[0].wait()

    @pl.loop(0, chunks)
    def _(q):
        row = q * batch

        @pl.when(q < chunks - 1)
        def _():
            fill(row + batch)

        total = taps(lambda di: wide_ref[:, pl.ds(row + di, batch)], conv_ref.at[0])
        x = x_ref[:, pl.ds(row, batch)].astype(jnp.float32).reshape(members * flat, channels)
        y = gated(x, total).reshape(members, batch, groups, 8, channels)
        parts = swap_strips(
            [y[:, i].reshape(members * groups, 8, channels) for i in range(batch)], width
        )
        for j in range(batch):
            part = parts[j].astype(jnp.bfloat16).reshape(members, groups, 8, channels)
            for k in range(groups):
                send_ref[q, k * batch + j] = part[:, k]
        exchange(
            lambda d: send_ref.at[q, d],
            recv_ref.at[q, me],
            me,
            devices,
            send_sem.at[q],
            recv_sem.at[q],
        )

    head_of_row = lax.broadcasted_iota(jnp.int32, ones_ref.shape, 0) // everyone
    head_of_lane = lax.broadcasted_iota(jnp.int32, ones_ref.shape, 1) // (channels // HEADS)
    ones_ref[...] = jnp.where(head_of_row == head_of_lane, 1.0, 0.0).astype(jnp.bfloat16)
    edge = jnp.zeros((1, width, everyone, 3 * channels), jnp.bfloat16)
    wide2_ref[0:1] = edge
    wide2_ref[rows + 1 : rows + 2] = edge

    @pl.when(me == 0)
    def _():
        left_ref[...] = jnp.zeros_like(left_ref)

    @pl.when(me == devices - 1)
    def _():
        right_ref[...] = jnp.zeros_like(right_ref)

    def to_right(q):
        span = pl.ds(q * batch, batch)
        return pltpu.make_async_remote_copy(
            src_ref=state_ref.at[span, width - 1],
            dst_ref=left_ref.at[span],
            send_sem=edge_send.at[0, q],
            recv_sem=edge_recv.at[0, q],
            device_id={"mem": lax.rem(me + 1, devices)},
            device_id_type=pl.DeviceIdType.MESH,
        )

    def to_left(q):
        span = pl.ds(q * batch, batch)
        return pltpu.make_async_remote_copy(
            src_ref=state_ref.at[span, 0],
            dst_ref=right_ref.at[span],
            send_sem=edge_send.at[1, q],
            recv_sem=edge_recv.at[1, q],
            device_id={"mem": lax.rem(me + devices - 1, devices)},
            device_id_type=pl.DeviceIdType.MESH,
        )

    def fill2(q):
        @pl.when(me > 0)
        def _():
            to_right(q).wait_recv()

        @pl.when(me < devices - 1)
        def _():
            to_left(q).wait_recv()

        for step in range(batch):
            row = q * batch + step
            for col in range(-1, width + 1):
                if col < 0:
                    x = left_ref[row]
                elif col == width:
                    x = right_ref[row]
                else:
                    x = state_ref[row, col]
                value = normalised(x.astype(jnp.float32), gain_ref[1, 0:1]).astype(jnp.bfloat16)
                for dj in range(3):
                    target = col + 1 - dj
                    if 0 <= target < width:
                        wide2_ref[row + 1, target, :, dj * channels : (dj + 1) * channels] = value

    @pl.loop(0, chunks + 2)
    def _(q):
        @pl.when(q < chunks)
        def _():
            wait_all(recv_ref.at[q, 0], me, devices, recv_sem.at[q], True)
            x = recv_ref[q].astype(jnp.float32).reshape(everyone, 8, channels)
            x = jnp.transpose(x, (1, 0, 2))
            y = attend_block(x, gain_ref[0, 1:2], qkv_ref[0], out_w_ref[0], ones_ref)
            y = y.astype(jnp.bfloat16).reshape(batch, width, everyone, channels)
            state_ref[pl.ds(q * batch, batch)] = y

            @pl.when(me < devices - 1)
            def _():
                to_right(q).start()

            @pl.when(me > 0)
            def _():
                to_left(q).start()

        @pl.when(q == 1)
        def _():
            loads[1].wait()

        @pl.when((q >= 1) & (q <= chunks))
        def _():
            fill2(q - 1)

        @pl.when(q >= 2)
        def _():
            p = q - 2
            row = p * batch
            total = taps(lambda di: wide2_ref[pl.ds(row + di, batch)], conv_ref.at[1])
            x = state_ref[pl.ds(row, batch)].astype(jnp.float32).reshape(-1, channels)
            x = gated(x, total).astype(jnp.bfloat16).astype(jnp.float32)
            x = x.reshape(8, everyone, channels)
            y = attend_block(x, gain_ref[1, 1:2], qkv_ref[1], out_w_ref[1], ones_ref)
            y = jnp.transpose(y, (1, 0, 2)).astype(jnp.bfloat16)
            send2_ref[p] = y.reshape(devices, members, 8, channels)
            exchange(
                lambda d: send2_ref.at[p, d],
                recv2_ref.at[p, me],
                me,
                devices,
                send2_sem.at[p],
                recv2_sem.at[p],
            )

    @pl.loop(0, chunks)
    def _(q):
        wait_all(send_ref.at[q, 0], me, devices, send_sem.at[q], False)

        @pl.when(me < devices - 1)
        def _():
            to_right(q).wait_send()

        @pl.when(me > 0)
        def _():
            to_left(q).wait_send()

    @pl.loop(0, chunks)
    def _(q):
        wait_all(recv2_ref.at[q, 0], me, devices, recv2_sem.at[q], True)
        parts = []
        for j in range(batch):
            part = [recv2_ref[q, k * batch + j].astype(jnp.float32) for k in range(groups)]
            parts.append(jnp.concatenate(part, axis=0))
        for i, part in enumerate(swap_strips(parts, width)):
            part = part.reshape(groups, members, 8, channels)
            for member in range(members):
                line = jnp.concatenate([part[k, member] for k in range(groups)], axis=0)
                out_ref[member, q * batch + i] = line.astype(jnp.bfloat16)

    @pl.loop(0, chunks)
    def _(q):
        wait_all(send2_ref.at[q, 0], me, devices, send2_sem.at[q], False)


def body(field, norm_gain, conv_weight, qkv_weight, out_weight):
    members, rows, cols, channels = field.shape
    devices = lax.axis_size("mem")
    width = cols // devices
    chunks = rows * width // 8
    everyone = members * devices
    vmem = lambda *shape: pltpu.VMEM(shape, jnp.bfloat16)
    block = vmem(chunks, devices, members, 8, channels)
    sems = pltpu.SemaphoreType.DMA((chunks, devices))
    edges = pltpu.SemaphoreType.DMA((2, chunks))
    here = pl.BlockSpec(memory_space=pltpu.VMEM)
    return pl.pallas_call(
        functools.partial(kernel, devices),
        in_specs=[here, here, pl.BlockSpec(memory_space=pl.ANY), here, here],
        out_specs=here,
        out_shape=jax.ShapeDtypeStruct(field.shape, jnp.bfloat16),
        scratch_shapes=[
            vmem(*conv_weight.shape),
            vmem(HEADS * everyone, channels),
            vmem(members, rows + 2, cols, 3 * channels),
            vmem(rows + 2, width, everyone, 3 * channels),
            vmem(rows, width, everyone, channels),
            vmem(rows, everyone, channels),
            vmem(rows, everyone, channels),
            block,
            block,
            block,
            block,
            pltpu.SemaphoreType.DMA((2,)),
            sems,
            sems,
            sems,
            sems,
            edges,
            edges,
        ],
        compiler_params=pltpu.CompilerParams(
            vmem_limit_bytes=VMEM_LIMIT, collective_id=0, has_side_effects=True
        ),
        name="transformer",
    )(field, norm_gain, conv_weight, qkv_weight, out_weight)


def solution(mesh):
    return jax.shard_map(
        body,
        mesh=mesh,
        in_specs=(P(("grp", "mem"), None, None, None), P(), P(), P(), P()),
        out_specs=P(("grp", "mem"), None, None, None),
        check_vma=False,
    )
```

time: 173 us -> 133 us (0.77)
  Pallas kernels: 151 us -> 129 us
  local copies, waits for them, and re-layouts: 15.2 us -> 3.16 us
  starting transfers between devices: 4.36 us -> 0 us
    pallas_call x3 -> x1, Pallas kernels: 151 us -> 129 us  [body(): pl.pallas_call(functools.partial(kernel, devices), in_specs=[here, here,...]
    slice x2 -> x0, local copies, waits for them, and re-layouts: 6.19 us -> none  [the longest x1 4.91 us: body(): grid = conv_cell(grid, left, right, norm_gain[1, 0], conv_weight[1])]
    ppermute x2 -> x0, starting transfers between devices: 4.36 us -> none  [the longest x1 3.06 us: body(): left = lax.ppermute(grid[:, -1:], 'mem', forward)]
    squeeze x2 -> x0, local copies, waits for them, and re-layouts: 3.71 us -> none  [the longest x1 2.04 us: body(): qkv_weight[1]]
    unnamed x5 -> x1, local copies, waits for them, and re-layouts: 3.96 us -> 3.16 us
  transfers between devices with their start and end apart: 2 -> 0, of which waited for: 1 -> 0; matrix products, arithmetic and copies ran while one was open for 0% -> 0% of each run, Pallas kernels for 0% -> 0%
where the time goes in v2:
time: 133 us; the launch traced here: 132 us
  Pallas kernels  129 us (97%)
  local copies, waits for them, and re-layouts  3.16 us (2%)
    pallas_call x1, Pallas kernels, body(): pl.pallas_call(functools.partial(kernel, devices), in_specs=[here, here,...  129 us
    unnamed x1, local copies, waits for them, and re-layouts  3.16 us

profile of v2, /device:TPU:0, one launch (start us, length us, event | category | flops | bytes accessed | tf_op | source)
XLA Modules:
  0.0 132.4 jit_solution(4854804735416755264)
XLA Ops:
  0.0 129.2 %transformer.1 = bf16[4,16,64,256]{3,2,1,0:T(8,128)(2,1)} custom-call(bf16[4,16,64,256]{3,2,1,0:T(8,128)(2,1)} %x_ref.1, f32[2,2,256]{2,1,0:T(2,128)} %gain_ref.1, bf16[2,3,3,256,512]{4,3,2,1,0:T(8,128)(2,1)} %conv_hbm.1, bf16[2,256,768]{2,1,0:T(8,128)(2,1)} %qkv_ref.1, bf16[2,256,256]{2,1,0:T(8,128)(2,1)} %out_w_ref.1), custom_call_target="tpu_custom_call" | custom-call | tf_op jit(solution)/shard_map/transformer/pallas_call | solution.py:373
  129.2 3.2 %copy.7 = bf16[4,16,64,256]{3,2,1,0:T(8,128)(2,1)} copy(bf16[4,16,64,256]{3,2,1,0:T(8,128)(2,1)} %transformer.1) | data formatting | bytes 4194304

commit v3 on v2

--- a/solution.py
+++ b/solution.py
@@ -1,4 +1,5 @@
 import functools
+import math
 
 import jax
 import jax.numpy as jnp
@@ -9,6 +10,8 @@
 
 HEADS = 8
 epsilon = 1e-06
+OUTWARD = 2
+HOMEWARD = 2
 VMEM_LIMIT = 58 * 1024 * 1024
 
 
@@ -167,6 +170,8 @@
     chunks = rows // batch
     groups = cols // 8
     everyone = members * devices
+    pair = send_ref.shape[2]
+    pair2 = send2_ref.shape[2]
     me = lax.axis_index("mem")
     flat = batch * cols
     column = lax.broadcasted_iota(jnp.int32, (flat, channels), 0) % cols
@@ -211,15 +216,19 @@
         for j in range(batch):
             part = parts[j].astype(jnp.bfloat16).reshape(members, groups, 8, channels)
             for k in range(groups):
-                send_ref[q, k * batch + j] = part[:, k]
-        exchange(
-            lambda d: send_ref.at[q, d],
-            recv_ref.at[q, me],
-            me,
-            devices,
-            send_sem.at[q],
-            recv_sem.at[q],
-        )
+                send_ref[q // pair, k * batch + j, q % pair] = part[:, k]
+
+        @pl.when(q % pair == pair - 1)
+        def _():
+            g = q // pair
+            exchange(
+                lambda d: send_ref.at[g, d],
+                recv_ref.at[g, me],
+                me,
+                devices,
+                send_sem.at[g],
+                recv_sem.at[g],
+            )
 
     head_of_row = lax.broadcasted_iota(jnp.int32, ones_ref.shape, 0) // everyone
     head_of_lane = lax.broadcasted_iota(jnp.int32, ones_ref.shape, 1) // (channels // HEADS)
@@ -286,8 +295,13 @@
     def _(q):
         @pl.when(q < chunks)
         def _():
-            wait_all(recv_ref.at[q, 0], me, devices, recv_sem.at[q], True)
-            x = recv_ref[q].astype(jnp.float32).reshape(everyone, 8, channels)
+            g = q // pair
+
+            @pl.when(q % pair == 0)
+            def _():
+                wait_all(recv_ref.at[g, 0], me, devices, recv_sem.at[g], True)
+
+            x = recv_ref[g, :, q % pair].astype(jnp.float32).reshape(everyone, 8, channels)
             x = jnp.transpose(x, (1, 0, 2))
             y = attend_block(x, gain_ref[0, 1:2], qkv_ref[0], out_w_ref[0], ones_ref)
             y = y.astype(jnp.bfloat16).reshape(batch, width, everyone, channels)
@@ -319,20 +333,26 @@
             x = x.reshape(8, everyone, channels)
             y = attend_block(x, gain_ref[1, 1:2], qkv_ref[1], out_w_ref[1], ones_ref)
             y = jnp.transpose(y, (1, 0, 2)).astype(jnp.bfloat16)
-            send2_ref[p] = y.reshape(devices, members, 8, channels)
-            exchange(
-                lambda d: send2_ref.at[p, d],
-                recv2_ref.at[p, me],
-                me,
-                devices,
-                send2_sem.at[p],
-                recv2_sem.at[p],
-            )
+            g = p // pair2
+            send2_ref[g, :, p % pair2] = y.reshape(devices, members, 8, channels)
+
+            @pl.when(p % pair2 == pair2 - 1)
+            def _():
+                exchange(
+                    lambda d: send2_ref.at[g, d],
+                    recv2_ref.at[g, me],
+                    me,
+                    devices,
+                    send2_sem.at[g],
+                    recv2_sem.at[g],
+                )
+
+    @pl.loop(0, chunks // pair)
+    def _(g):
+        wait_all(send_ref.at[g, 0], me, devices, send_sem.at[g], False)
 
     @pl.loop(0, chunks)
     def _(q):
-        wait_all(send_ref.at[q, 0], me, devices, send_sem.at[q], False)
-
         @pl.when(me < devices - 1)
         def _():
             to_right(q).wait_send()
@@ -343,10 +363,15 @@
 
     @pl.loop(0, chunks)
     def _(q):
-        wait_all(recv2_ref.at[q, 0], me, devices, recv2_sem.at[q], True)
+        g = q // pair2
+
+        @pl.when(q % pair2 == 0)
+        def _():
+            wait_all(recv2_ref.at[g, 0], me, devices, recv2_sem.at[g], True)
+
         parts = []
         for j in range(batch):
-            part = [recv2_ref[q, k * batch + j].astype(jnp.float32) for k in range(groups)]
+            part = [recv2_ref[g, k * batch + j, q % pair2].astype(jnp.float32) for k in range(groups)]
             parts.append(jnp.concatenate(part, axis=0))
         for i, part in enumerate(swap_strips(parts, width)):
             part = part.reshape(groups, members, 8, channels)
@@ -354,9 +379,9 @@
                 line = jnp.concatenate([part[k, member] for k in range(groups)], axis=0)
                 out_ref[member, q * batch + i] = line.astype(jnp.bfloat16)
 
-    @pl.loop(0, chunks)
-    def _(q):
-        wait_all(send2_ref.at[q, 0], me, devices, send2_sem.at[q], False)
+    @pl.loop(0, chunks // pair2)
+    def _(g):
+        wait_all(send2_ref.at[g, 0], me, devices, send2_sem.at[g], False)
 
 
 def body(field, norm_gain, conv_weight, qkv_weight, out_weight):
@@ -366,8 +391,11 @@
     chunks = rows * width // 8
     everyone = members * devices
     vmem = lambda *shape: pltpu.VMEM(shape, jnp.bfloat16)
-    block = vmem(chunks, devices, members, 8, channels)
-    sems = pltpu.SemaphoreType.DMA((chunks, devices))
+    pair, pair2 = math.gcd(OUTWARD, chunks), math.gcd(HOMEWARD, chunks)
+    block = vmem(chunks // pair, devices, pair, members, 8, channels)
+    block2 = vmem(chunks // pair2, devices, pair2, members, 8, channels)
+    sems = pltpu.SemaphoreType.DMA((chunks // pair, devices))
+    sems2 = pltpu.SemaphoreType.DMA((chunks // pair2, devices))
     edges = pltpu.SemaphoreType.DMA((2, chunks))
     here = pl.BlockSpec(memory_space=pltpu.VMEM)
     return pl.pallas_call(
@@ -385,13 +413,13 @@
             vmem(rows, everyone, channels),
             block,
             block,
-            block,
-            block,
+            block2,
+            block2,
             pltpu.SemaphoreType.DMA((2,)),
             sems,
             sems,
-            sems,
-            sems,
+            sems2,
+            sems2,
             edges,
             edges,
         ],

time: 133 us -> 130 us (0.977)
  Pallas kernels: 129 us -> 127 us
    pallas_call x1, Pallas kernels: 129 us -> 127 us  [body(): pl.pallas_call(functools.partial(kernel, devices), in_specs=[here, here,...]
where the time goes in v3:
time: 130 us
  Pallas kernels  127 us (98%)
  local copies, waits for them, and re-layouts  3.16 us (2%)
    pallas_call x1, Pallas kernels, body(): pl.pallas_call(functools.partial(kernel, devices), in_specs=[here, here,...  127 us
    unnamed x1, local copies, waits for them, and re-layouts  3.16 us

profile of v3, /device:TPU:0, one launch (start us, length us, event | category | flops | bytes accessed | tf_op | source)
XLA Modules:
  0.0 129.8 jit_solution(1295751243312157883)
XLA Ops:
  0.0 126.6 %transformer.1 = bf16[4,16,64,256]{3,2,1,0:T(8,128)(2,1)} custom-call(bf16[4,16,64,256]{3,2,1,0:T(8,128)(2,1)} %x_ref.1, f32[2,2,256]{2,1,0:T(2,128)} %gain_ref.1, bf16[2,3,3,256,512]{4,3,2,1,0:T(8,128)(2,1)} %conv_hbm.1, bf16[2,256,768]{2,1,0:T(8,128)(2,1)} %qkv_ref.1, bf16[2,256,256]{2,1,0:T(8,128)(2,1)} %out_w_ref.1), custom_call_target="tpu_custom_call" | custom-call | tf_op jit(solution)/shard_map/transformer/pallas_call | solution.py:401
  126.6 3.2 %copy.7 = bf16[4,16,64,256]{3,2,1,0:T(8,128)(2,1)} copy(bf16[4,16,64,256]{3,2,1,0:T(8,128)(2,1)} %transformer.1) | data formatting | bytes 4194304

commit v4 on v3

--- a/solution.py
+++ b/solution.py
@@ -293,28 +293,6 @@
 
     @pl.loop(0, chunks + 2)
     def _(q):
-        @pl.when(q < chunks)
-        def _():
-            g = q // pair
-
-            @pl.when(q % pair == 0)
-            def _():
-                wait_all(recv_ref.at[g, 0], me, devices, recv_sem.at[g], True)
-
-            x = recv_ref[g, :, q % pair].astype(jnp.float32).reshape(everyone, 8, channels)
-            x = jnp.transpose(x, (1, 0, 2))
-            y = attend_block(x, gain_ref[0, 1:2], qkv_ref[0], out_w_ref[0], ones_ref)
-            y = y.astype(jnp.bfloat16).reshape(batch, width, everyone, channels)
-            state_ref[pl.ds(q * batch, batch)] = y
-
-            @pl.when(me < devices - 1)
-            def _():
-                to_right(q).start()
-
-            @pl.when(me > 0)
-            def _():
-                to_left(q).start()
-
         @pl.when(q == 1)
         def _():
             loads[1].wait()
@@ -346,6 +324,28 @@
                     send2_sem.at[g],
                     recv2_sem.at[g],
                 )
+
+        @pl.when(q < chunks)
+        def _():
+            g = q // pair
+
+            @pl.when(q % pair == 0)
+            def _():
+                wait_all(recv_ref.at[g, 0], me, devices, recv_sem.at[g], True)
+
+            x = recv_ref[g, :, q % pair].astype(jnp.float32).reshape(everyone, 8, channels)
+            x = jnp.transpose(x, (1, 0, 2))
+            y = attend_block(x, gain_ref[0, 1:2], qkv_ref[0], out_w_ref[0], ones_ref)
+            y = y.astype(jnp.bfloat16).reshape(batch, width, everyone, channels)
+            state_ref[pl.ds(q * batch, batch)] = y
+
+            @pl.when(me < devices - 1)
+            def _():
+                to_right(q).start()
+
+            @pl.when(me > 0)
+            def _():
+                to_left(q).start()
 
     @pl.loop(0, chunks // pair)
     def _(g):

time: 130 us -> 156 us (1.20)
  Pallas kernels: 127 us -> 153 us
    pallas_call x1, Pallas kernels: 127 us -> 153 us  [body(): pl.pallas_call(functools.partial(kernel, devices), in_specs=[here, here,...]
where the time goes in v4:
time: 156 us
  Pallas kernels  153 us (98%)
  local copies, waits for them, and re-layouts  3.16 us (2%)
    pallas_call x1, Pallas kernels, body(): pl.pallas_call(functools.partial(kernel, devices), in_specs=[here, here,...  153 us
    unnamed x1, local copies, waits for them, and re-layouts  3.16 us

profile of v4, /device:TPU:0, one launch (start us, length us, event | category | flops | bytes accessed | tf_op | source)
XLA Modules:
  0.0 156.0 jit_solution(13446160882023985754)
XLA Ops:
  0.0 152.9 %transformer.1 = bf16[4,16,64,256]{3,2,1,0:T(8,128)(2,1)} custom-call(bf16[4,16,64,256]{3,2,1,0:T(8,128)(2,1)} %x_ref.1, f32[2,2,256]{2,1,0:T(2,128)} %gain_ref.1, bf16[2,3,3,256,512]{4,3,2,1,0:T(8,128)(2,1)} %conv_hbm.1, bf16[2,256,768]{2,1,0:T(8,128)(2,1)} %qkv_ref.1, bf16[2,256,256]{2,1,0:T(8,128)(2,1)} %out_w_ref.1), custom_call_target="tpu_custom_call" | custom-call | tf_op jit(solution)/shard_map/transformer/pallas_call | solution.py:401
  152.9 3.2 %copy.7 = bf16[4,16,64,256]{3,2,1,0:T(8,128)(2,1)} copy(bf16[4,16,64,256]{3,2,1,0:T(8,128)(2,1)} %transformer.1) | data formatting | bytes 4194304
